TPU v7x, 32 devices: a whole 2x2x4 slice. The times are simulated.
32 devices in a mesh: mem: 4 (over x, core), slab: 8 (over z, y).
Axes of the slice: x: 2, y: 2, z: 4, core: 2. Of those that a mesh axis runs over, the one named last changes fastest.
Arguments:
- anomalies: bfloat16 [8, 4096, 4096], P('mem', 'slab'), may hold values from -2.390625 to 2.390625
- increment: float32 [4096, 4096], P('slab'), may hold values from -6 to 6
- spectrum: float32 [4096, 4096], P(None, 'slab'), may hold values from 0.01 to 2, as said below
Outputs:
- product: float32 [4096, 4096], P('slab')
Inputs may be any that keep to these rules, and one draw needn't show every extreme that they name: spectrum[k, l] equals spectrum[(4096 - k) % 4096, (4096 - l) % 4096], and is positive.
All inputs are finite; a program needn't handle non-finite values.
Results may differ from a plain program's by a relative error of at most 0.0003.
Values sent between devices are 32-bit elements; how exact they have to be, the bound alone decides.
A program may use at most 192 MiB of HBM per device.

v0:
```python
import math
import jax
import jax.numpy as jnp
from jax import lax
from jax.sharding import PartitionSpec as P


def dft_tables(length, sign):
    first = 1 << (length.bit_length() - 1) // 2
    second = length // first
    index_a = jnp.arange(first, dtype=jnp.int32)
    index_b = jnp.arange(second, dtype=jnp.int32)
    angle_first = (
        2.0 * math.pi / first * (index_a[:, None] * index_a[None, :] % first).astype(jnp.float32)
    )
    angle_twist = (
        2.0 * math.pi / length * (index_a[:, None] * index_b[None, :] % length).astype(jnp.float32)
    )
    angle_second = (
        2.0 * math.pi / second * (index_b[:, None] * index_b[None, :] % second).astype(jnp.float32)
    )
    return (
        first,
        jnp.cos(angle_first),
        sign * jnp.sin(angle_first),
        jnp.cos(angle_twist),
        sign * jnp.sin(angle_twist),
        jnp.cos(angle_second),
        sign * jnp.sin(angle_second),
    )


def complex_section(form, real_part, imag_part, mat_cos, mat_sin):
    highest = lax.Precision.HIGHEST
    out_real = jnp.einsum(form, real_part, mat_cos, precision=highest)
    out_real = out_real - jnp.einsum(form, imag_part, mat_sin, precision=highest)
    out_imag = jnp.einsum(form, real_part, mat_sin, precision=highest)
    out_imag = out_imag + jnp.einsum(form, imag_part, mat_cos, precision=highest)
    return (out_real, out_imag)


def transform(real_part, imag_part, factors, along_last):
    first, first_cos, first_sin, twist_cos, twist_sin, second_cos, second_sin = factors
    shape = real_part.shape
    if along_last:
        blocked = (shape[0], shape[1], first, shape[2] // first)
        form_one, form_two = ("mrab,ac->mrcb", "mrcb,bd->mrdc")
        tw_cos, tw_sin = (twist_cos, twist_sin)
    else:
        blocked = (shape[0], first, shape[1] // first, shape[2])
        form_one, form_two = ("mabk,ac->mcbk", "mcbk,bd->mdck")
        tw_cos, tw_sin = (twist_cos[:, :, None], twist_sin[:, :, None])
    real_part = real_part.reshape(blocked)
    imag_part = imag_part.reshape(blocked)
    step_real, step_imag = complex_section(form_one, real_part, imag_part, first_cos, first_sin)
    twist_real = step_real * tw_cos - step_imag * tw_sin
    twist_imag = step_real * tw_sin + step_imag * tw_cos
    out_real, out_imag = complex_section(form_two, twist_real, twist_imag, second_cos, second_sin)
    out_real = out_real.reshape(shape)
    out_imag = out_imag.reshape(shape)
    return (out_real, out_imag)


def per_device(anomalies, increment, spectrum):
    col_count = anomalies.shape[2]
    row_total = spectrum.shape[0]
    forward_y = dft_tables(col_count, -1.0)
    inverse_y = dft_tables(col_count, 1.0)
    forward_x = dft_tables(row_total, -1.0)
    inverse_x = dft_tables(row_total, 1.0)
    scaled = spectrum * (1.0 / (row_total * col_count))
    fields = anomalies * increment[None]
    wave_real, wave_imag = transform(fields[0::2], fields[1::2], forward_y, True)
    part_real, part_imag = transform(
        lax.all_to_all(wave_real, "slab", split_axis=2, concat_axis=1, tiled=True),
        lax.all_to_all(wave_imag, "slab", split_axis=2, concat_axis=1, tiled=True),
        forward_x,
        False,
    )
    part_real = part_real * scaled[None]
    part_imag = part_imag * scaled[None]
    part_real, part_imag = transform(part_real, part_imag, inverse_x, False)
    back_real = lax.all_to_all(part_real, "slab", split_axis=1, concat_axis=2, tiled=True)
    back_imag = lax.all_to_all(part_imag, "slab", split_axis=1, concat_axis=2, tiled=True)
    even_part, odd_part = transform(back_real, back_imag, inverse_y, True)
    total = jnp.sum(anomalies[0::2] * even_part + anomalies[1::2] * odd_part, axis=0)
    return lax.psum(total, "mem")


def solution(mesh):
    placed = (P("mem", "slab", None), P("slab", None), P(None, "slab"))
    return jax.shard_map(
        per_device, mesh=mesh, in_specs=placed, out_specs=P("slab", None), check_vma=False
    )
```

profile of v0, /device:TPU:0, one launch (start us, length us, event | category | flops | bytes accessed | tf_op | source)
XLA Modules:
  0.0 1516.1 jit_solution(14172679125190159585)
XLA Ops:
  86.5 24.8 %fusion.6 = (f32[512,64,64]{0,1,2:T(8,128)}, f32[512,64,64]{0,1,2:T(8,128)}) fusion(f32[64,64]{0,1:T(8,128)S(1)} %get-tuple-element.17, f32[64,64]{0,1:T(8,128)S(1)} %get-tuple-element.18, f32[64,512,64]{1,0,2:T(8,128)} %fusion.69, f32[64,512,64]{1,0,2:T(8,128)} %fusion.65, f32[64,512,64]{1,0,2:T(8,128)} %fusion.67, f32[512,64,64]{0,2,1:T(8,128)} %bitcast.203), kind=kOutput, calls=%fused_computation.17 | convolution fusion | flops 1627447296 | bytes 50364416 | tf_op jit(solution)/shard_map/mrab,ac->mrcb/dot_general | solution.py:35
  111.3 16.5 %fusion.57 = f32[64,512,64]{1,0,2:T(8,128)S(1)} fusion(f32[512,64,64]{0,1,2:T(8,128)} %get-tuple-element.12), kind=kOutput, calls=%fused_computation.78 | convolution fusion | flops 1610670080 | bytes 16777216 | tf_op jit(solution)/shard_map/mrcb,bd->mrdc/dot_general | solution.py:38
  144.8 22.8 %copy.138 = f32[1,512,4096]{1,0,2:T(1,128)} copy(f32[1,512,4096]{1,2,0:T(8,128)S(1)} %bitcast.204) | data formatting | bytes 16777216 | tf_op jit(solution)/shard_map/reshape | solution.py:60
  191.6 17.2 %subtract_bitcast_fusion.1 = f32[1,512,64,64]{1,2,3,0:T(8,128)S(1)} fusion(f32[64,512,64]{1,0,2:T(8,128)S(1)} %fusion.59, f32[512,64,64]{0,1,2:T(8,128)} %get-tuple-element.11), kind=kOutput, calls=%fused_computation.29 | convolution fusion | flops 1612767232 | bytes 25165824 | tf_op jit(solution)/shard_map/mrcb,bd->mrdc/dot_general | solution.py:35
  213.7 22.8 %copy.132 = f32[1,512,4096]{1,0,2:T(1,128)} copy(f32[1,512,4096]{1,2,0:T(8,128)S(1)} %bitcast.205) | data formatting | bytes 16777216 | tf_op jit(solution)/shard_map/reshape | solution.py:59
  236.5 121.8 %all-to-all-done.1 = f32[1,512,4096]{1,0,2:T(1,128)} async-done(((f32[1,512,4096]{1,0,2:T(1,128)}), f32[1,512,4096]{1,0,2:T(1,128)}, u32[]{:S(2)}, u32[]{:S(2)}) %all-to-all-start.1) | async-done | bytes 8388640 | tf_op jit(solution)/shard_map/all_to_all | solution.py:76
  380.4 17.8 %fusion.49 = f32[64,64,512]{2,0,1:T(8,128)} fusion(f32[64,64,512]{2,1,0:T(8,128)} %bitcast.190), kind=kOutput, calls=%fused_computation.70 | convolution fusion | flops 1610670080 | bytes 16777216 | tf_op jit(solution)/shard_map/mabk,ac->mcbk/dot_general | solution.py:38
  411.7 134.0 %all-to-all-done = f32[1,512,4096]{1,0,2:T(1,128)} async-done(((f32[1,512,4096]{1,0,2:T(1,128)}), f32[1,512,4096]{1,0,2:T(1,128)}, u32[]{:S(2)}, u32[]{:S(2)}) %all-to-all-start) | async-done | bytes 8388640 | tf_op jit(solution)/shard_map/all_to_all | solution.py:75
  562.5 18.1 %fusion.55 = f32[64,64,512]{2,0,1:T(8,128)} fusion(f32[64,64,512]{2,1,0:T(8,128)} %bitcast.196), kind=kOutput, calls=%fused_computation.76 | convolution fusion | flops 1610670080 | bytes 16777216 | tf_op jit(solution)/shard_map/mabk,ac->mcbk/dot_general | solution.py:35
  580.6 24.6 %multiply_subtract_fusion.1 = (f32[64,64,512]{2,0,1:T(8,128)}, f32[64,64,512]{2,0,1:T(8,128)}) fusion(f32[64,64]{0,1:T(8,128)S(1)} %get-tuple-element.17, f32[64,64]{0,1:T(8,128)S(1)} %get-tuple-element.18, f32[64,64,512]{2,0,1:T(8,128)} %fusion.49, f32[64,64,512]{2,0,1:T(8,128)} %fusion.55, f32[64,64,512]{2,0,1:T(8,128)} %fusion.51, ...), kind=kOutput, calls=%fused_computation.27 | convolution fusion | flops 1627451392 | bytes 50364416 | tf_op jit(solution)/shard_map/mabk,ac->mcbk/dot_general | solution.py:37
  605.2 18.4 %fusion.43 = f32[64,64,512]{2,0,1:T(8,128)} fusion(f32[64,64,512]{2,0,1:T(8,128)} %get-tuple-element.10), kind=kOutput, calls=%fused_computation.64 | convolution fusion | flops 1610674176 | bytes 16777216 | tf_op jit(solution)/shard_map/mcbk,bd->mdck/dot_general | solution.py:36
  742.1 24.8 %multiply_subtract_fusion = (f32[64,64,512]{2,0,1:T(8,128)}, f32[64,64,512]{2,0,1:T(8,128)}) fusion(f32[64,64]{0,1:T(8,128)S(1)} %fusion.152, f32[64,64]{0,1:T(8,128)S(1)} %get-tuple-element.18, f32[64,64,512]{2,0,1:T(8,128)} %fusion.33, f32[64,64,512]{2,0,1:T(8,128)} %fusion.39, f32[64,64,512]{2,0,1:T(8,128)} %fusion.35, f32[64,64,512]{2,1,0:T(8,128)} %bitcast.186), kind=kOutput, calls=%fused_computation.25 | convolution fusion | flops 1627447296 | bytes 50364416 | tf_op jit(solution)/shard_map/mabk,ac->mcbk/dot_general | solution.py:37
  766.9 16.5 %fusion.25 = f32[64,64,512]{2,0,1:T(8,128)S(1)} fusion(f32[64,64,512]{2,0,1:T(8,128)} %get-tuple-element.8), kind=kOutput, calls=%fused_computation.46 | convolution fusion | flops 1610670080 | bytes 16777216 | tf_op jit(solution)/shard_map/mcbk,bd->mdck/dot_general | solution.py:38
  800.5 22.8 %copy.162 = f32[1,4096,512]{2,0,1:T(1,128)} copy(f32[1,4096,512]{2,1,0:T(8,128)S(1)} %bitcast.208) | data formatting | bytes 16777216 | tf_op jit(solution)/shard_map/reshape | solution.py:60
  828.5 16.3 %fusion.27 = f32[64,64,512]{2,0,1:T(8,128)S(1)} fusion(f32[64,64,512]{2,0,1:T(8,128)} %get-tuple-element.8), kind=kOutput, calls=%fused_computation.48 | convolution fusion | flops 1610670080 | bytes 16777216 | tf_op jit(solution)/shard_map/mcbk,bd->mdck/dot_general | solution.py:36
  844.8 17.2 %fusion.83 = f32[64,64,512]{2,0,1:T(8,128)S(1)} fusion(f32[64,64,512]{2,0,1:T(8,128)S(1)} %fusion.27, f32[64,64,512]{2,0,1:T(8,128)} %get-tuple-element.7), kind=kOutput, calls=%fused_computation.96 | convolution fusion | flops 1612767232 | bytes 25165824 | tf_op jit(solution)/shard_map/mcbk,bd->mdck/dot_general | solution.py:35
  866.9 22.8 %copy.156 = f32[1,4096,512]{2,0,1:T(1,128)} copy(f32[1,4096,512]{2,1,0:T(8,128)S(1)} %bitcast.209) | data formatting | bytes 16777216 | tf_op jit(solution)/shard_map/reshape | solution.py:59
  889.7 120.7 %all-to-all-done.3 = f32[1,4096,512]{2,0,1:T(1,128)} async-done(((f32[1,4096,512]{2,0,1:T(1,128)}), f32[1,4096,512]{2,0,1:T(1,128)}, u32[]{:S(2)}, u32[]{:S(2)}) %all-to-all-start.3) | async-done | bytes 8388640 | tf_op jit(solution)/shard_map/all_to_all | solution.py:84
  1032.4 17.8 %fusion.17 = f32[64,512,64]{1,0,2:T(8,128)} fusion(f32[512,64,64]{0,2,1:T(8,128)} %bitcast.192), kind=kOutput, calls=%fused_computation.38 | convolution fusion | flops 1610670080 | bytes 16777216 | tf_op jit(solution)/shard_map/mrab,ac->mrcb/dot_general | solution.py:38
  1063.5 134.1 %all-to-all-done.2 = f32[1,4096,512]{2,0,1:T(1,128)} async-done(((f32[1,4096,512]{2,0,1:T(1,128)}), f32[1,4096,512]{2,0,1:T(1,128)}, u32[]{:S(2)}, u32[]{:S(2)}) %all-to-all-start.2) | async-done | bytes 8388640 | tf_op jit(solution)/shard_map/all_to_all | solution.py:83
  1214.4 18.1 %fusion.21 = f32[64,512,64]{1,0,2:T(8,128)} fusion(f32[512,64,64]{0,2,1:T(8,128)} %bitcast.194), kind=kOutput, calls=%fused_computation.42 | convolution fusion | flops 1610670080 | bytes 16777216 | tf_op jit(solution)/shard_map/mrab,ac->mrcb/dot_general | solution.py:37
  1232.4 24.5 %fusion.2 = (f32[512,64,64]{0,1,2:T(8,128)}, f32[512,64,64]{0,1,2:T(8,128)}) fusion(f32[64,64]{0,1:T(8,128)S(1)} %fusion.152, f32[64,64]{0,1:T(8,128)S(1)} %get-tuple-element.18, f32[64,512,64]{1,0,2:T(8,128)} %fusion.21, f32[64,512,64]{1,0,2:T(8,128)} %fusion.17, f32[64,512,64]{1,0,2:T(8,128)} %fusion.19, f32[512,64,64]{0,2,1:T(8,128)} %bitcast.195), kind=kOutput, calls=%fused_computation.7 | convolution fusion | flops 1627447296 | bytes 50364416 | tf_op jit(solution)/shard_map/mrab,ac->mrcb/dot_general | solution.py:35
  1257.0 17.0 %fusion.11 = f32[64,512,64]{1,0,2:T(8,128)S(1)} fusion(f32[512,64,64]{0,1,2:T(8,128)} %get-tuple-element.6), kind=kOutput, calls=%fused_computation.32 | convolution fusion | flops 1610670080 | bytes 16777216 | tf_op jit(solution)/shard_map/mrcb,bd->mrdc/dot_general | solution.py:36
  1347.9 152.2 %all-reduce.2.cloned.1.call-done = f32[512,4096]{0,1:T(8,128)} async-done(((f32[512,4096]{0,1:T(8,128)}), f32[512,4096]{0,1:T(8,128)}) %all-reduce.2.cloned.1.call-update) | async-done | bytes 8388624 | tf_op jit(solution)/shard_map/psum | solution.py:87
  (84 shorter events, 458.5 us)
Async XLA Ops:
  46.7 26.6 %copy-start.6 = (f32[1,512,4096]{1,2,0:T(8,128)}, f32[1,512,4096]{1,2,0:T(8,128)S(1)}, u32[]{:S(2)}) copy-start(f32[1,512,4096]{1,2,0:T(8,128)S(1)} %get-tuple-element.14) | copy-start | bytes 25165828
  111.3 16.5 %copy-start = (f32[512,64,64]{0,1,2:T(8,128)S(1)}, f32[512,64,64]{0,1,2:T(8,128)}, u32[]{:S(2)}) copy-start(f32[512,64,64]{0,1,2:T(8,128)} %get-tuple-element.11) | copy-start | bytes 25165828
  167.6 190.7 %all-to-all-start.1 = ((f32[1,512,4096]{1,0,2:T(1,128)}), f32[1,512,4096]{1,0,2:T(1,128)}, u32[]{:S(2)}, u32[]{:S(2)}) async-start(f32[1,512,4096]{1,0,2:T(1,128)} %copy.138), calls=%async_computation.1 | async-start | bytes 16777216 | tf_op jit(solution)/shard_map/all_to_all | solution.py:76
  358.3 187.4 %all-to-all-start = ((f32[1,512,4096]{1,0,2:T(1,128)}), f32[1,512,4096]{1,0,2:T(1,128)}, u32[]{:S(2)}, u32[]{:S(2)}) async-start(f32[1,512,4096]{1,0,2:T(1,128)} %copy.132), calls=%async_computation | async-start | bytes 16777216 | tf_op jit(solution)/shard_map/all_to_all | solution.py:75
  380.4 17.8 %copy-start.2 = (f32[1,8,512,512]{3,2,1,0:T(8,128)S(1)}, f32[1,8,512,512]{3,2,1,0:T(8,128)}, u32[]{:S(2)}) copy-start(f32[1,8,512,512]{3,2,1,0:T(8,128)} %copy.139) | copy-start | bytes 25165828
  605.2 18.4 %copy-start.5 = (f32[64,64,512]{2,0,1:T(8,128)S(1)}, f32[64,64,512]{2,0,1:T(8,128)}, u32[]{:S(2)}) copy-start(f32[64,64,512]{2,0,1:T(8,128)} %get-tuple-element.10) | copy-start | bytes 25165828
  605.2 30.9 %slice-start.2 = ((s8[8388608]{0:T(1024)(128)(4,1)}), s8[4194304]{0:T(1024)(128)(4,1)S(1)}, s32[]{:S(2)}) async-start(s8[8388608]{0:T(1024)(128)(4,1)} %bitcast.182), calls=%async_computation.7 | async-start | bytes 8388608
  623.6 12.5 slice-start.3
  702.3 26.5 %slice-start.4 = ((s8[8388608]{0:T(1024)(128)(4,1)}), s8[4194304]{0:T(1024)(128)(4,1)S(1)}, s32[]{:S(2)}) async-start(s8[8388608]{0:T(1024)(128)(4,1)} %bitcast.187), calls=%async_computation.9 | async-start | bytes 8388608
  715.6 13.3 slice-start.5
  766.9 16.5 %copy-start.1 = (f32[64,64,512]{2,0,1:T(8,128)S(1)}, f32[64,64,512]{2,0,1:T(8,128)}, u32[]{:S(2)}) copy-start(f32[64,64,512]{2,0,1:T(8,128)} %get-tuple-element.7) | copy-start | bytes 25165828
  823.3 187.2 %all-to-all-start.3 = ((f32[1,4096,512]{2,0,1:T(1,128)}), f32[1,4096,512]{2,0,1:T(1,128)}, u32[]{:S(2)}, u32[]{:S(2)}) async-start(f32[1,4096,512]{2,0,1:T(1,128)} %copy.162), calls=%async_computation.3 | async-start | bytes 16777216 | tf_op jit(solution)/shard_map/all_to_all | solution.py:84
  1010.4 187.2 %all-to-all-start.2 = ((f32[1,4096,512]{2,0,1:T(1,128)}), f32[1,4096,512]{2,0,1:T(1,128)}, u32[]{:S(2)}, u32[]{:S(2)}) async-start(f32[1,4096,512]{2,0,1:T(1,128)} %copy.156), calls=%async_computation.2 | async-start | bytes 16777216 | tf_op jit(solution)/shard_map/all_to_all | solution.py:83
  1015.4 484.7 %all-reduce.2.cloned.1.call-start = ((), (), s32[]{:S(2)}) async-start(), calls=%async_computation.4 | async-start | bytes 16777216 | tf_op jit(solution)/shard_map/psum | solution.py:87
  1032.4 17.8 %copy-start.3 = (f32[1,512,8,512]{1,3,2,0:T(8,128)S(1)}, f32[1,512,8,512]{1,3,2,0:T(8,128)}, u32[]{:S(2)}) copy-start(f32[1,512,8,512]{1,3,2,0:T(8,128)} %copy.163) | copy-start | bytes 25165828
  1256.9 17.0 %copy-start.4 = (f32[512,64,64]{0,1,2:T(8,128)S(1)}, f32[512,64,64]{0,1,2:T(8,128)}, u32[]{:S(2)}) copy-start(f32[512,64,64]{0,1,2:T(8,128)} %get-tuple-element.6) | copy-start | bytes 25165828
  1256.9 30.6 %slice-start = ((s8[8388608]{0:T(1024)(128)(4,1)}), s8[4194304]{0:T(1024)(128)(4,1)S(1)}, s32[]{:S(2)}) async-start(s8[8388608]{0:T(1024)(128)(4,1)} %bitcast.180), calls=%async_computation.5 | async-start | bytes 8388608
  1274.0 13.5 slice-start.1
  1301.3 39.0 %slice-start.6 = ((s8[8388608]{0:T(1024)(128)(4,1)}), s8[4194304]{0:T(1024)(128)(4,1)S(1)}, s32[]{:S(2)}) async-start(s8[8388608]{0:T(1024)(128)(4,1)} %bitcast.200), calls=%async_computation.11 | async-start | bytes 8388608
  1313.0 27.3 %slice-start.7 = ((s8[8388608]{0:T(1024)(128)(4,1)}), s8[4194304]{0:T(1024)(128)(4,1)S(1)}, s32[]{:S(2)}) async-start(s8[8388608]{0:T(1024)(128)(4,1)} %bitcast.200), calls=%async_computation.12 | async-start | bytes 8388608
  1328.6 11.7 copy-start.7
Sparse Core Ops, SparseCore 0:
  1348.0 152.0 all-reduce.1
where the time goes:
time: 1520 us
  waiting for transfers between devices  663 us (44%)
  matrix products  521 us (34%)
  local copies, waits for them, and re-layouts  261 us (17%)
  other arithmetic  33.7 us (2%)
  starting transfers between devices  23 us (2%)
    psum x1, waiting for transfers between devices, per_device(): return lax.psum(total, 'mem')  152 us
    dot_general x8, matrix products, complex_section(): out_real = jnp.einsum(form, real_part, mat_cos, precision=highest)  144 us
    dot_general x8, matrix products, complex_section(): out_imag = jnp.einsum(form, real_part, mat_sin, precision=highest)  134 us
    all_to_all x1, waiting for transfers between devices, per_device(): lax.all_to_all(part_real, 'slab', split_axis=1, concat_axis=2, tiled=True)  134 us
    all_to_all x1, waiting for transfers between devices, per_device(): lax.all_to_all(wave_real, 'slab', split_axis=2, concat_axis=1, tiled=True)  134 us
    all_to_all x1, waiting for transfers between devices, per_device(): lax.all_to_all(wave_imag, 'slab', split_axis=2, concat_axis=1, tiled=True)  122 us
    dot_general x8, matrix products, complex_section(): jnp.einsum(form, imag_part, mat_sin, precision=highest)  121 us
    dot_general x8, matrix products, complex_section(): jnp.einsum(form, imag_part, mat_cos, precision=highest)  121 us
  transfers between devices with their start and end apart: 5, of which 5 were waited for; matrix products, arithmetic and copies ran while one was open for 14% of the time, Pallas kernels for 0%

commit v1 on v0

--- a/solution.py
+++ b/solution.py
@@ -80,7 +80,12 @@
     part_real = part_real * scaled[None]
     part_imag = part_imag * scaled[None]
     part_real, part_imag = transform(part_real, part_imag, inverse_x, False)
-    back_real = lax.all_to_all(part_real, "slab", split_axis=1, concat_axis=2, tiled=True)
+    back_real = jnp.concatenate(
+        lax.all_to_all(
+            jnp.stack(jnp.split(part_real, lax.axis_size("slab"), axis=1)), "slab", 0, 0
+        ),
+        axis=2,
+    )
     back_imag = lax.all_to_all(part_imag, "slab", split_axis=1, concat_axis=2, tiled=True)
     even_part, odd_part = transform(back_real, back_imag, inverse_y, True)
     total = jnp.sum(anomalies[0::2] * even_part + anomalies[1::2] * odd_part, axis=0)

time: 1520 us -> 1520 us (level)
  local copies, waits for them, and re-layouts: 261 us -> 239 us
    reshape x2 -> x1, local copies, waits for them, and re-layouts: 45.6 us -> 22.8 us  [transform(): out_real = out_real.reshape(shape)]
    unnamed x38 -> x44, local copies, waits for them, and re-layouts: 51.5 us -> 51.2 us
where the time goes in v1:
time: 1520 us; the launch traced here: 1510 us
  waiting for transfers between devices  677 us (45%)
  matrix products  522 us (34%)
  local copies, waits for them, and re-layouts  239 us (16%)
  other arithmetic  33.7 us (2%)
  starting transfers between devices  23 us (2%)
    psum x1, waiting for transfers between devices, per_device(): return lax.psum(total, 'mem')  152 us
    dot_general x8, matrix products, complex_section(): out_real = jnp.einsum(form, real_part, mat_cos, precision=highest)  145 us
    all_to_all x1, waiting for transfers between devices, per_device(): lax.all_to_all(part_imag, 'slab', split_axis=1, concat_axis=2, tiled=True)  135 us
    all_to_all x1, waiting for transfers between devices, per_device(): lax.all_to_all(wave_real, 'slab', split_axis=2, concat_axis=1, tiled=True)  134 us
    dot_general x8, matrix products, complex_section(): out_imag = jnp.einsum(form, real_part, mat_sin, precision=highest)  134 us
    all_to_all x1, waiting for transfers between devices, per_device(): lax.all_to_all(jnp.stack(jnp.split(part_real, lax.axis_size('slab'), axis...  134 us
    all_to_all x1, waiting for transfers between devices, per_device(): lax.all_to_all(wave_imag, 'slab', split_axis=2, concat_axis=1, tiled=True)  122 us
    dot_general x8, matrix products, complex_section(): jnp.einsum(form, imag_part, mat_sin, precision=highest)  122 us
  transfers between devices with their start and end apart: 5, of which 5 were waited for; matrix products, arithmetic and copies ran while one was open for 14% of the time, Pallas kernels for 0%

profile of v1, /device:TPU:0, one launch (start us, length us, event | category | flops | bytes accessed | tf_op | source)
XLA Modules:
  0.0 1508.9 jit_solution(3775833564742034415)
XLA Ops:
  86.5 24.8 %fusion.6 = (f32[512,64,64]{0,1,2:T(8,128)}, f32[512,64,64]{0,1,2:T(8,128)}) fusion(f32[64,64]{0,1:T(8,128)S(1)} %get-tuple-element.17, f32[64,64]{0,1:T(8,128)S(1)} %get-tuple-element.18, f32[64,512,64]{1,0,2:T(8,128)} %fusion.69, f32[64,512,64]{1,0,2:T(8,128)} %fusion.65, f32[64,512,64]{1,0,2:T(8,128)} %fusion.67, f32[512,64,64]{0,2,1:T(8,128)} %bitcast.233), kind=kOutput, calls=%fused_computation.17 | convolution fusion | flops 1627447296 | bytes 50364416 | tf_op jit(solution)/shard_map/mrab,ac->mrcb/dot_general | solution.py:35
  111.4 16.5 %fusion.57 = f32[64,512,64]{1,0,2:T(8,128)S(1)} fusion(f32[512,64,64]{0,1,2:T(8,128)} %get-tuple-element.12), kind=kOutput, calls=%fused_computation.78 | convolution fusion | flops 1610670080 | bytes 16777216 | tf_op jit(solution)/shard_map/mrcb,bd->mrdc/dot_general | solution.py:38
  144.9 22.8 %copy.138 = f32[1,512,4096]{1,0,2:T(1,128)} copy(f32[1,512,4096]{1,2,0:T(8,128)S(1)} %bitcast.242) | data formatting | bytes 16777216 | tf_op jit(solution)/shard_map/reshape | solution.py:60
  175.3 16.3 %fusion.59 = f32[64,512,64]{1,0,2:T(8,128)S(1)} fusion(f32[512,64,64]{0,1,2:T(8,128)} %get-tuple-element.12), kind=kOutput, calls=%fused_computation.80 | convolution fusion | flops 1610674176 | bytes 16777216 | tf_op jit(solution)/shard_map/mrcb,bd->mrdc/dot_general | solution.py:36
  191.7 17.2 %subtract_bitcast_fusion.1 = f32[1,512,64,64]{1,2,3,0:T(8,128)S(1)} fusion(f32[64,512,64]{1,0,2:T(8,128)S(1)} %fusion.59, f32[512,64,64]{0,1,2:T(8,128)} %get-tuple-element.11), kind=kOutput, calls=%fused_computation.29 | convolution fusion | flops 1612767232 | bytes 25165824 | tf_op jit(solution)/shard_map/mrcb,bd->mrdc/dot_general | solution.py:35
  213.8 22.8 %copy.132 = f32[1,512,4096]{1,0,2:T(1,128)} copy(f32[1,512,4096]{1,2,0:T(8,128)S(1)} %bitcast.243) | data formatting | bytes 16777216 | tf_op jit(solution)/shard_map/reshape | solution.py:59
  236.6 121.8 %all-to-all-done.1 = f32[1,512,4096]{1,0,2:T(1,128)} async-done(((f32[1,512,4096]{1,0,2:T(1,128)}), f32[1,512,4096]{1,0,2:T(1,128)}, u32[]{:S(2)}, u32[]{:S(2)}) %all-to-all-start.1) | async-done | bytes 8388640 | tf_op jit(solution)/shard_map/all_to_all | solution.py:76
  380.5 17.8 %fusion.49 = f32[64,64,512]{2,0,1:T(8,128)} fusion(f32[64,64,512]{2,1,0:T(8,128)} %bitcast.220), kind=kOutput, calls=%fused_computation.70 | convolution fusion | flops 1610670080 | bytes 16777216 | tf_op jit(solution)/shard_map/mabk,ac->mcbk/dot_general | solution.py:38
  411.8 134.0 %all-to-all-done = f32[1,512,4096]{1,0,2:T(1,128)} async-done(((f32[1,512,4096]{1,0,2:T(1,128)}), f32[1,512,4096]{1,0,2:T(1,128)}, u32[]{:S(2)}, u32[]{:S(2)}) %all-to-all-start) | async-done | bytes 8388640 | tf_op jit(solution)/shard_map/all_to_all | solution.py:75
  562.6 18.1 %fusion.55 = f32[64,64,512]{2,0,1:T(8,128)} fusion(f32[64,64,512]{2,1,0:T(8,128)} %bitcast.226), kind=kOutput, calls=%fused_computation.76 | convolution fusion | flops 1610670080 | bytes 16777216 | tf_op jit(solution)/shard_map/mabk,ac->mcbk/dot_general | solution.py:35
  580.7 24.6 %multiply_subtract_fusion.1 = (f32[64,64,512]{2,0,1:T(8,128)}, f32[64,64,512]{2,0,1:T(8,128)}) fusion(f32[64,64]{0,1:T(8,128)S(1)} %get-tuple-element.17, f32[64,64]{0,1:T(8,128)S(1)} %get-tuple-element.18, f32[64,64,512]{2,0,1:T(8,128)} %fusion.49, f32[64,64,512]{2,0,1:T(8,128)} %fusion.55, f32[64,64,512]{2,0,1:T(8,128)} %fusion.51, ...), kind=kOutput, calls=%fused_computation.27 | convolution fusion | flops 1627451392 | bytes 50364416 | tf_op jit(solution)/shard_map/mabk,ac->mcbk/dot_general | solution.py:37
  605.3 18.4 %fusion.43 = f32[64,64,512]{2,0,1:T(8,128)} fusion(f32[64,64,512]{2,0,1:T(8,128)} %get-tuple-element.10), kind=kOutput, calls=%fused_computation.64 | convolution fusion | flops 1610674176 | bytes 16777216 | tf_op jit(solution)/shard_map/mcbk,bd->mdck/dot_general | solution.py:36
  742.2 24.8 %multiply_subtract_fusion = (f32[64,64,512]{2,0,1:T(8,128)}, f32[64,64,512]{2,0,1:T(8,128)}) fusion(f32[64,64]{0,1:T(8,128)S(1)} %fusion.160, f32[64,64]{0,1:T(8,128)S(1)} %get-tuple-element.18, f32[64,64,512]{2,0,1:T(8,128)} %fusion.33, f32[64,64,512]{2,0,1:T(8,128)} %fusion.39, f32[64,64,512]{2,0,1:T(8,128)} %fusion.35, f32[64,64,512]{2,1,0:T(8,128)} %bitcast.216), kind=kOutput, calls=%fused_computation.25 | convolution fusion | flops 1627447296 | bytes 50364416 | tf_op jit(solution)/shard_map/mabk,ac->mcbk/dot_general | solution.py:37
  767.0 16.5 %fusion.25 = f32[64,64,512]{2,0,1:T(8,128)S(1)} fusion(f32[64,64,512]{2,0,1:T(8,128)} %get-tuple-element.8), kind=kOutput, calls=%fused_computation.46 | convolution fusion | flops 1610670080 | bytes 16777216 | tf_op jit(solution)/shard_map/mcbk,bd->mdck/dot_general | solution.py:38
  800.6 22.8 %copy.161 = f32[1,4096,512]{2,0,1:T(1,128)} copy(f32[1,4096,512]{2,1,0:T(8,128)S(1)} %bitcast.246) | data formatting | bytes 16777216 | tf_op jit(solution)/shard_map/reshape | solution.py:60
  828.6 16.3 %fusion.27 = f32[64,64,512]{2,0,1:T(8,128)S(1)} fusion(f32[64,64,512]{2,0,1:T(8,128)} %get-tuple-element.8), kind=kOutput, calls=%fused_computation.48 | convolution fusion | flops 1610670080 | bytes 16777216 | tf_op jit(solution)/shard_map/mcbk,bd->mdck/dot_general | solution.py:36
  844.9 17.7 %fusion.83 = f32[64,64,512]{2,0,1:T(8,128)S(1)} fusion(f32[64,64,512]{2,0,1:T(8,128)S(1)} %fusion.27, f32[64,64,512]{2,0,1:T(8,128)} %get-tuple-element.7), kind=kOutput, calls=%fused_computation.96 | convolution fusion | flops 1612767232 | bytes 25165824 | tf_op jit(solution)/shard_map/mcbk,bd->mdck/dot_general | solution.py:35
  875.9 134.6 %all-to-all-done.3 = f32[1,4096,512]{2,0,1:T(1,128)} async-done(((f32[1,4096,512]{2,0,1:T(1,128)}), f32[1,4096,512]{2,0,1:T(1,128)}, u32[]{:S(2)}, u32[]{:S(2)}) %all-to-all-start.3) | async-done | bytes 8388640 | tf_op jit(solution)/shard_map/all_to_all | solution.py:89
  1032.5 17.8 %fusion.17 = f32[64,512,64]{1,0,2:T(8,128)} fusion(f32[512,64,64]{0,2,1:T(8,128)} %bitcast.222), kind=kOutput, calls=%fused_computation.38 | convolution fusion | flops 1610670080 | bytes 16777216 | tf_op jit(solution)/shard_map/mrab,ac->mrcb/dot_general | solution.py:38
  1063.8 133.9 %all-to-all-done.2 = f32[8,1,512,512]{3,2,1,0:T(8,128)} async-done(((f32[8,1,512,512]{3,2,1,0:T(8,128)}), f32[8,1,512,512]{3,2,1,0:T(8,128)}, u32[]{:S(2)}, u32[]{:S(2)}) %all-to-all-start.2) | async-done | bytes 8388640 | tf_op jit(solution)/shard_map/all_to_all | solution.py:84
  1206.8 17.8 %fusion.21 = f32[64,512,64]{1,0,2:T(8,128)} fusion(f32[512,64,64]{0,2,1:T(8,128)} %bitcast.224), kind=kOutput, calls=%fused_computation.42 | convolution fusion | flops 1610670080 | bytes 16777216 | tf_op jit(solution)/shard_map/mrab,ac->mrcb/dot_general | solution.py:37
  1224.6 24.9 %fusion.2 = (f32[512,64,64]{0,1,2:T(8,128)}, f32[512,64,64]{0,1,2:T(8,128)}) fusion(f32[64,64]{0,1:T(8,128)S(1)} %fusion.160, f32[64,64]{0,1:T(8,128)S(1)} %get-tuple-element.18, f32[64,512,64]{1,0,2:T(8,128)} %fusion.21, f32[64,512,64]{1,0,2:T(8,128)} %fusion.17, f32[64,512,64]{1,0,2:T(8,128)} %fusion.19, f32[512,64,64]{0,2,1:T(8,128)} %bitcast.225), kind=kOutput, calls=%fused_computation.7 | convolution fusion | flops 1627447296 | bytes 50364416 | tf_op jit(solution)/shard_map/mrab,ac->mrcb/dot_general | solution.py:35
  1249.5 17.0 %fusion.11 = f32[64,512,64]{1,0,2:T(8,128)S(1)} fusion(f32[512,64,64]{0,1,2:T(8,128)} %get-tuple-element.6), kind=kOutput, calls=%fused_computation.32 | convolution fusion | flops 1610670080 | bytes 16777216 | tf_op jit(solution)/shard_map/mrcb,bd->mrdc/dot_general | solution.py:36
  1340.4 152.3 %all-reduce.2.cloned.1.call-done = f32[512,4096]{0,1:T(8,128)} async-done(((f32[512,4096]{0,1:T(8,128)}), f32[512,4096]{0,1:T(8,128)}) %all-reduce.2.cloned.1.call-update) | async-done | bytes 8388624 | tf_op jit(solution)/shard_map/psum | solution.py:92
  (90 shorter events, 443.1 us)
Async XLA Ops:
  46.7 26.6 %copy-start.6 = (f32[1,512,4096]{1,2,0:T(8,128)}, f32[1,512,4096]{1,2,0:T(8,128)S(1)}, u32[]{:S(2)}) copy-start(f32[1,512,4096]{1,2,0:T(8,128)S(1)} %get-tuple-element.14) | copy-start | bytes 25165828
  111.4 16.5 %copy-start = (f32[512,64,64]{0,1,2:T(8,128)S(1)}, f32[512,64,64]{0,1,2:T(8,128)}, u32[]{:S(2)}) copy-start(f32[512,64,64]{0,1,2:T(8,128)} %get-tuple-element.11) | copy-start | bytes 25165828
  167.7 190.7 %all-to-all-start.1 = ((f32[1,512,4096]{1,0,2:T(1,128)}), f32[1,512,4096]{1,0,2:T(1,128)}, u32[]{:S(2)}, u32[]{:S(2)}) async-start(f32[1,512,4096]{1,0,2:T(1,128)} %copy.138), calls=%async_computation.1 | async-start | bytes 16777216 | tf_op jit(solution)/shard_map/all_to_all | solution.py:76
  358.4 187.4 %all-to-all-start = ((f32[1,512,4096]{1,0,2:T(1,128)}), f32[1,512,4096]{1,0,2:T(1,128)}, u32[]{:S(2)}, u32[]{:S(2)}) async-start(f32[1,512,4096]{1,0,2:T(1,128)} %copy.132), calls=%async_computation | async-start | bytes 16777216 | tf_op jit(solution)/shard_map/all_to_all | solution.py:75
  380.5 17.8 %copy-start.2 = (f32[1,8,512,512]{3,2,1,0:T(8,128)S(1)}, f32[1,8,512,512]{3,2,1,0:T(8,128)}, u32[]{:S(2)}) copy-start(f32[1,8,512,512]{3,2,1,0:T(8,128)} %copy.139) | copy-start | bytes 25165828
  605.3 18.4 %copy-start.5 = (f32[64,64,512]{2,0,1:T(8,128)S(1)}, f32[64,64,512]{2,0,1:T(8,128)}, u32[]{:S(2)}) copy-start(f32[64,64,512]{2,0,1:T(8,128)} %get-tuple-element.10) | copy-start | bytes 25165828
  605.3 30.9 %slice-start.2 = ((s8[8388608]{0:T(1024)(128)(4,1)}), s8[4194304]{0:T(1024)(128)(4,1)S(1)}, s32[]{:S(2)}) async-start(s8[8388608]{0:T(1024)(128)(4,1)} %bitcast.212), calls=%async_computation.7 | async-start | bytes 8388608
  623.7 12.5 slice-start.3
  702.4 26.5 %slice-start.4 = ((s8[8388608]{0:T(1024)(128)(4,1)}), s8[4194304]{0:T(1024)(128)(4,1)S(1)}, s32[]{:S(2)}) async-start(s8[8388608]{0:T(1024)(128)(4,1)} %bitcast.217), calls=%async_computation.9 | async-start | bytes 8388608
  715.6 13.3 slice-start.5
  767.0 16.5 %copy-start.1 = (f32[64,64,512]{2,0,1:T(8,128)S(1)}, f32[64,64,512]{2,0,1:T(8,128)}, u32[]{:S(2)}) copy-start(f32[64,64,512]{2,0,1:T(8,128)} %get-tuple-element.7) | copy-start | bytes 25165828
  823.4 187.1 %all-to-all-start.3 = ((f32[1,4096,512]{2,0,1:T(1,128)}), f32[1,4096,512]{2,0,1:T(1,128)}, u32[]{:S(2)}, u32[]{:S(2)}) async-start(f32[1,4096,512]{2,0,1:T(1,128)} %copy.161), calls=%async_computation.3 | async-start | bytes 16777216 | tf_op jit(solution)/shard_map/all_to_all | solution.py:89
  1010.5 187.2 %all-to-all-start.2 = ((f32[8,1,512,512]{3,2,1,0:T(8,128)}), f32[8,1,512,512]{3,2,1,0:T(8,128)}, u32[]{:S(2)}, u32[]{:S(2)}) async-start(f32[8,1,512,512]{3,2,1,0:T(8,128)} %fusion.93), calls=%async_computation.2 | async-start | bytes 16777216 | tf_op jit(solution)/shard_map/all_to_all | solution.py:84
  1015.5 477.1 %all-reduce.2.cloned.1.call-start = ((), (), s32[]{:S(2)}) async-start(), calls=%async_computation.4 | async-start | bytes 16777216 | tf_op jit(solution)/shard_map/psum | solution.py:92
  1032.5 17.8 %copy-start.3 = (f32[1,512,8,512]{1,3,2,0:T(8,128)S(1)}, f32[1,512,8,512]{1,3,2,0:T(8,128)}, u32[]{:S(2)}) copy-start(f32[1,512,8,512]{1,3,2,0:T(8,128)} %copy.162) | copy-start | bytes 25165828
  1249.5 17.0 %copy-start.4 = (f32[512,64,64]{0,1,2:T(8,128)S(1)}, f32[512,64,64]{0,1,2:T(8,128)}, u32[]{:S(2)}) copy-start(f32[512,64,64]{0,1,2:T(8,128)} %get-tuple-element.6) | copy-start | bytes 25165828
  1249.5 30.4 %slice-start = ((s8[8388608]{0:T(1024)(128)(4,1)}), s8[4194304]{0:T(1024)(128)(4,1)S(1)}, s32[]{:S(2)}) async-start(s8[8388608]{0:T(1024)(128)(4,1)} %bitcast.210), calls=%async_computation.5 | async-start | bytes 8388608
  1266.5 13.4 slice-start.1
  1293.7 39.1 %slice-start.6 = ((s8[8388608]{0:T(1024)(128)(4,1)}), s8[4194304]{0:T(1024)(128)(4,1)S(1)}, s32[]{:S(2)}) async-start(s8[8388608]{0:T(1024)(128)(4,1)} %bitcast.230), calls=%async_computation.11 | async-start | bytes 8388608
  1305.4 27.4 %slice-start.7 = ((s8[8388608]{0:T(1024)(128)(4,1)}), s8[4194304]{0:T(1024)(128)(4,1)S(1)}, s32[]{:S(2)}) async-start(s8[8388608]{0:T(1024)(128)(4,1)} %bitcast.230), calls=%async_computation.12 | async-start | bytes 8388608
  1321.1 11.7 copy-start.7
Sparse Core Ops, SparseCore 0:
  1340.5 152.0 all-reduce.1
